TPU v7x, 32 devices: a whole 2x2x4 slice. The times are simulated.
32 devices in a mesh: row: 4 (over z), col: 8 (over y, x, core).
Axes of the slice: x: 2, y: 2, z: 4, core: 2. Of those that a mesh axis runs over, the one named last changes fastest.
Arguments:
- rho_real: float32 [4, 8, 1280000], P('row', 'col'), as said below
- rho_imag: float32 [4, 8, 1280000], P('row', 'col'), as said below
- cav_real: float32 [100, 100], replicated, may hold values from -0.4375 to 0.4375
- cav_imag: float32 [100, 100], replicated, may hold values from -0.4375 to 0.4375
- mech_real: float32 [64, 64], replicated, may hold values from -0.5 to 0.5
- mech_imag: float32 [64, 64], replicated, may hold values from -0.5 to 0.5
Outputs:
- out_real: float32 [4, 8, 1280000], P('row', 'col')
- out_imag: float32 [4, 8, 1280000], P('row', 'col')
Inputs may be any that keep to these rules, and one draw needn't show every extreme that they name: rho_real is the real part of a Hermitian matrix: symmetric in the whole matrix's row and column index. rho_imag is the imaginary part of a Hermitian matrix: antisymmetric in the whole matrix's row and column index.
All inputs are finite; a program needn't handle non-finite values.
Results may differ from a plain program's by a relative error of at most 0.0001.
Values sent between devices are 32-bit elements; how exact they have to be, the bound alone decides.
No kernel may reach another device: no remote copies, remote signals or barrier semaphores. Data moves between devices by JAX's collectives and lax.ppermute only.
A program may use at most 192 MiB of HBM per device.

v0:
```python
import jax
import jax.numpy as jnp
from jax import lax
from jax.sharding import PartitionSpec as P

MECH = 64
highest = lax.Precision.HIGHEST


def cavity_sides(parts, cav_real, cav_imag):
    real_part, imag_part = parts
    left_real = jnp.einsum("cd,mdne->mcne", cav_real, real_part, precision=highest) - jnp.einsum(
        "cd,mdne->mcne", cav_imag, imag_part, precision=highest
    )
    left_imag = jnp.einsum("cd,mdne->mcne", cav_real, imag_part, precision=highest) + jnp.einsum(
        "cd,mdne->mcne", cav_imag, real_part, precision=highest
    )
    right_real = jnp.einsum("mcne,fe->mcnf", left_real, cav_real, precision=highest) + jnp.einsum(
        "mcne,fe->mcnf", left_imag, cav_imag, precision=highest
    )
    right_imag = jnp.einsum("mcne,fe->mcnf", left_imag, cav_real, precision=highest) - jnp.einsum(
        "mcne,fe->mcnf", left_real, cav_imag, precision=highest
    )
    return (right_real, right_imag)


def mech_mix(pieces, mech_real, mech_imag, adjoint):
    real_part, imag_part = pieces
    plain_rr = jnp.einsum("mn,nok->mok", mech_real, real_part, precision=highest)
    plain_ii = jnp.einsum("mn,nok->mok", mech_imag, imag_part, precision=highest)
    plain_ri = jnp.einsum("mn,nok->mok", mech_real, imag_part, precision=highest)
    plain_ir = jnp.einsum("mn,nok->mok", mech_imag, real_part, precision=highest)
    if adjoint:
        return (plain_rr + plain_ii, plain_ri - plain_ir)
    return (plain_rr - plain_ii, plain_ri + plain_ir)


def ket_side(parts, mech_real, mech_imag):
    real_part, imag_part = parts
    local_rows, cav_count, local_cols, width = real_part.shape
    groups = lax.axis_size("row")
    flat = cav_count * local_cols * width
    shaped = (
        real_part.reshape(local_rows, groups, flat // groups),
        imag_part.reshape(local_rows, groups, flat // groups),
    )
    mixed = mech_mix(
        (
            lax.all_to_all(shaped[0], "row", split_axis=1, concat_axis=0, tiled=True),
            lax.all_to_all(shaped[1], "row", split_axis=1, concat_axis=0, tiled=True),
        ),
        mech_real,
        mech_imag,
        False,
    )
    return (
        lax.all_to_all(mixed[0], "row", split_axis=0, concat_axis=1, tiled=True).reshape(
            local_rows, cav_count, local_cols, width
        ),
        lax.all_to_all(mixed[1], "row", split_axis=0, concat_axis=1, tiled=True).reshape(
            local_rows, cav_count, local_cols, width
        ),
    )


def bra_side(parts, mech_real, mech_imag):
    real_part, imag_part = parts
    local_rows, cav_count, local_cols, width = real_part.shape
    groups = lax.axis_size("col")
    flat = local_rows * cav_count * width
    moved_real = jnp.transpose(real_part, (2, 0, 1, 3)).reshape(local_cols, groups, flat // groups)
    moved_imag = jnp.transpose(imag_part, (2, 0, 1, 3)).reshape(local_cols, groups, flat // groups)
    mixed = mech_mix(
        (
            lax.all_to_all(moved_real, "col", split_axis=1, concat_axis=0, tiled=True),
            lax.all_to_all(moved_imag, "col", split_axis=1, concat_axis=0, tiled=True),
        ),
        mech_real,
        mech_imag,
        True,
    )
    back_real = jnp.transpose(
        lax.all_to_all(mixed[0], "col", split_axis=0, concat_axis=1, tiled=True).reshape(
            local_cols, local_rows, cav_count, width
        ),
        (1, 2, 0, 3),
    )
    back_imag = jnp.transpose(
        lax.all_to_all(mixed[1], "col", split_axis=0, concat_axis=1, tiled=True).reshape(
            local_cols, local_rows, cav_count, width
        ),
        (1, 2, 0, 3),
    )
    return (back_real, back_imag)


def local(rho_real, rho_imag, cav_real, cav_imag, mech_real, mech_imag):
    block_shape = rho_real.shape
    cav_count = cav_real.shape[0]
    local_rows = MECH // lax.axis_size("row")
    local_cols = MECH // lax.axis_size("col")
    shape_four = (local_rows, cav_count, local_cols, cav_count)
    state = (rho_real.reshape(shape_four), rho_imag.reshape(shape_four))
    state = cavity_sides(state, cav_real, cav_imag)
    state = bra_side(ket_side(state, mech_real, mech_imag), mech_real, mech_imag)
    return (state[0].reshape(block_shape), state[1].reshape(block_shape))


def solution(mesh):
    return jax.shard_map(
        local,
        mesh=mesh,
        in_specs=(P("row", "col", None), P("row", "col", None), P(), P(), P(), P()),
        out_specs=(P("row", "col", None), P("row", "col", None)),
        check_vma=False,
    )
```

profile of v0, /device:TPU:0, one launch (start us, length us, event | category | flops | bytes accessed | tf_op | source)
XLA Modules:
  0.0 1057.0 jit_solution(15498159880655077600)
XLA Ops:
  1.2 41.2 %reduce.7 = f32[1280000]{0:T(1024)} reduce(f32[1,1,1280000]{2,1,0:T(1,128)} %param.6, f32[]{:T(128)} %broadcast.6), dimensions={0,1}, to_apply=%param.6.reduce_sub_computation.3 | reduce | bytes 10240004 | tf_op args[0]
  42.4 14.0 %reshape.80 = f32[16,100,8,100]{3,2,1,0:T(8,128)} reshape(f32[1280000]{0:T(1024)} %reduce.7) | data formatting | bytes 10240000 | tf_op jit(solution)/shard_map/reshape | solution.py:103
  56.4 8.3 copy.58
  64.6 41.2 %reduce.6 = f32[1280000]{0:T(1024)} reduce(f32[1,1,1280000]{2,1,0:T(1,128)} %param.7, f32[]{:T(128)} %broadcast.6), dimensions={0,1}, to_apply=%param.7.reduce_sub_computation.3 | reduce | bytes 10240004 | tf_op args[1]
  105.9 14.1 %reshape.81 = f32[16,100,8,100]{3,2,1,0:T(8,128)} reshape(f32[1280000]{0:T(1024)} %reduce.6) | data formatting | bytes 10240000 | tf_op jit(solution)/shard_map/reshape | solution.py:103
  120.0 8.3 copy.59
  128.3 8.5 fusion.35
  136.8 5.8 fusion.32
  142.7 7.7 fusion.30
  150.4 5.8 fusion.38
  156.3 17.2 %fusion.6 = f32[16,100,8,100]{3,1,2,0:T(8,128)} fusion(f32[16,8,100,100]{3,2,1,0:T(8,128)S(1)} %fusion.35, f32[16,8,100,100]{3,2,1,0:T(8,128)} %fusion.30, f32[100,100]{1,0:T(8,128)S(1)} %copy-done.6), kind=kOutput, calls=%fused_computation.10 | convolution fusion | flops 1537280000 | bytes 15400000 | tf_op jit(solution)/shard_map/mcne,fe->mcnf/dot_general | solution.py:18
  173.5 13.6 %fusion.22 = f32[16,100,8,100]{3,1,2,0:T(8,128)S(1)} fusion(f32[16,100,8,100]{3,1,2,0:T(8,128)} %fusion.6, f32[16,8,100,100]{3,2,1,0:T(8,128)S(1)} %fusion.38, f32[16,8,100,100]{3,2,1,0:T(8,128)S(1)} %fusion.32, f32[100,100]{1,0:T(8,128)S(1)} %copy-done), kind=kOutput, calls=%fused_computation.30 | convolution fusion | flops 1538560000 | bytes 20520000 | tf_op jit(solution)/shard_map/mcne,fe->mcnf/dot_general | solution.py:18
  190.9 7.9 reshape.82
  198.9 5.1 copy.65
  204.0 6.8 all-to-all-start
  210.8 14.5 %fusion.4 = f32[16,100,8,100]{3,1,2,0:T(8,128)S(1)} fusion(f32[16,8,100,100]{3,2,1,0:T(8,128)} %copy-done.4, f32[16,8,100,100]{3,2,1,0:T(8,128)} %fusion.30, f32[100,100]{1,0:T(8,128)S(1)} %copy-done), kind=kOutput, calls=%fused_computation.8 | convolution fusion | flops 1537280000 | bytes 15400000 | tf_op jit(solution)/shard_map/mcne,fe->mcnf/dot_general | solution.py:21
  225.4 14.1 %fusion.25 = f32[16,100,8,100]{3,1,2,0:T(8,128)S(1)} fusion(f32[16,100,8,100]{3,1,2,0:T(8,128)S(1)} %fusion.4, f32[16,8,100,100]{3,2,1,0:T(8,128)} %copy-done.5, f32[16,8,100,100]{3,2,1,0:T(8,128)S(1)} %bitcast.139, f32[100,100]{1,0:T(8,128)S(1)} %copy-done.6), kind=kOutput, calls=%fused_computation.31 | convolution fusion | flops 1538560000 | bytes 20520000 | tf_op jit(solution)/shard_map/mcne,fe->mcnf/dot_general | solution.py:21
  243.3 7.9 reshape.84
  251.2 5.1 copy.69
  256.3 68.5 %all-to-all-done = f32[16,4,20000]{2,0,1:T(8,128)} async-done(((f32[16,4,20000]{2,0,1:T(8,128)}), f32[16,4,20000]{2,0,1:T(8,128)}, u32[]{:S(2)}, u32[]{:S(2)}) %all-to-all-start) | async-done | bytes 5120032 | tf_op jit(solution)/shard_map/all_to_all | solution.py:49
  324.8 5.1 all-to-all-start.1
  329.9 9.6 fusion.40
  339.4 103.5 %all-to-all-done.1 = f32[16,4,20000]{2,0,1:T(8,128)} async-done(((f32[16,4,20000]{2,0,1:T(8,128)}), f32[16,4,20000]{2,0,1:T(8,128)}, u32[]{:S(2)}, u32[]{:S(2)}) %all-to-all-start.1) | async-done | bytes 5120032 | tf_op jit(solution)/shard_map/all_to_all | solution.py:50
  442.9 11.1 %fusion = f32[64,1,20000]{2,0,1:T(8,128)} fusion(f32[20000,64]{0,1:T(8,128)} %fusion.40, f32[64,20000]{1,0:T(8,128)} %bitcast.13, f32[64,64]{1,0:T(8,128)S(1)} %copy-done.8), kind=kOutput, calls=%fused_computation.4 | convolution fusion | flops 984320000 | bytes 15376384 | tf_op jit(solution)/shard_map/mn,nok->mok/dot_general | solution.py:30
  454.0 10.2 copy.70
  464.3 5.0 all-to-all-start.2
  469.3 6.7 fusion.41
  476.0 9.6 fusion.1
  485.6 10.0 copy.74
  495.6 86.9 %all-to-all-done.2 = f32[64,1,20000]{2,1,0:T(1,128)} async-done(((f32[64,1,20000]{2,1,0:T(1,128)}), f32[64,1,20000]{2,1,0:T(1,128)}, u32[]{:S(2)}, u32[]{:S(2)}) %all-to-all-start.2) | async-done | bytes 5120032 | tf_op jit(solution)/shard_map/all_to_all | solution.py:57
  582.4 5.4 all-to-all-start.4
  587.9 6.7 copy.97
  594.6 8.6 reshape.86
  603.2 7.0 copy.72
  610.2 6.8 reshape.87
  617.0 5.7 copy.73
  622.7 78.3 %all-to-all-done.4 = f32[64,1,20000]{2,1,0:T(1,128)} async-done(((f32[64,1,20000]{2,1,0:T(1,128)}), f32[64,1,20000]{2,1,0:T(1,128)}, u32[]{:S(2)}, u32[]{:S(2)}) %all-to-all-start.4) | async-done | bytes 5120032 | tf_op jit(solution)/shard_map/all_to_all | solution.py:60
  701.0 4.7 all-to-all-start.3
  705.6 6.7 copy.96
  712.4 8.6 reshape.89
  721.0 7.0 copy.76
  728.0 6.9 reshape.90
  734.9 5.7 copy.77
  740.6 24.3 %all-to-all-done.3 = f32[8,8,20000]{2,0,1:T(8,128)} async-done(((f32[8,8,20000]{2,0,1:T(8,128)}), f32[8,8,20000]{2,0,1:T(8,128)}, u32[]{:S(2)}, u32[]{:S(2)}) %all-to-all-start.3) | async-done | bytes 5120032 | tf_op jit(solution)/shard_map/all_to_all | solution.py:75
  764.9 4.8 all-to-all-start.5
  769.8 9.5 fusion.13
  779.3 49.6 %all-to-all-done.5 = f32[8,8,20000]{2,0,1:T(8,128)} async-done(((f32[8,8,20000]{2,0,1:T(8,128)}), f32[8,8,20000]{2,0,1:T(8,128)}, u32[]{:S(2)}, u32[]{:S(2)}) %all-to-all-start.5) | async-done | bytes 5120032 | tf_op jit(solution)/shard_map/all_to_all | solution.py:76
  828.9 11.1 %fusion.2 = f32[64,1,20000]{2,0,1:T(8,128)} fusion(f32[20000,64]{0,1:T(8,128)} %fusion.13, f32[64,64]{1,0:T(8,128)S(1)} %copy-done.8, f32[8,8,20000]{2,0,1:T(8,128)} %all-to-all-done.5), kind=kOutput, calls=%fused_computation.6 | convolution fusion | flops 984320000 | bytes 15376384 | tf_op jit(solution)/shard_map/mn,nok->mok/dot_general | solution.py:30
  839.9 10.5 copy.78
  850.4 4.7 all-to-all-start.6
  855.1 6.7 fusion.15
  861.7 9.5 fusion.3
  871.3 10.1 copy.81
  881.3 33.0 %all-to-all-done.6 = f32[64,1,20000]{2,1,0:T(1,128)} async-done(((f32[64,1,20000]{2,1,0:T(1,128)}), f32[64,1,20000]{2,1,0:T(1,128)}, u32[]{:S(2)}, u32[]{:S(2)}) %all-to-all-start.6) | async-done | bytes 5120032 | tf_op jit(solution)/shard_map/all_to_all | solution.py:83
  914.3 4.7 all-to-all-start.7
  919.0 5.7 copy.95
  924.7 53.6 %all-to-all-done.7 = f32[64,1,20000]{2,1,0:T(1,128)} async-done(((f32[64,1,20000]{2,1,0:T(1,128)}), f32[64,1,20000]{2,1,0:T(1,128)}, u32[]{:S(2)}, u32[]{:S(2)}) %all-to-all-start.7) | async-done | bytes 5120032 | tf_op jit(solution)/shard_map/all_to_all | solution.py:89
  978.3 5.7 copy.94
  984.0 9.2 reshape.94
  993.2 9.5 copy.83
  1002.8 17.6 %reshape.95 = f32[1,1,1280000]{2,1,0:T(1,128)} reshape(f32[16,100,8,100]{3,2,1,0:T(8,128)} %copy.83) | data formatting | bytes 10240000 | tf_op jit(solution)/shard_map/reshape | solution.py:106
  1020.4 9.0 reshape.92
  1029.4 9.5 copy.80
  1038.9 17.7 %reshape.93 = f32[1,1,1280000]{2,1,0:T(1,128)} reshape(f32[16,100,8,100]{3,2,1,0:T(8,128)} %copy.80) | data formatting | bytes 10240000 | tf_op jit(solution)/shard_map/reshape | solution.py:106
  (31 shorter events, 8.3 us)
Async XLA Ops:
  0.6 127.6 %copy-start = (f32[100,100]{1,0:T(8,128)S(1)}, f32[100,100]{1,0:T(8,128)}, u32[]{:S(2)}) copy-start(f32[100,100]{1,0:T(8,128)} %param.8) | copy-start | bytes 120004
  128.3 8.5 copy-start.2
  128.3 8.5 copy-start.6
  128.3 14.4 %slice-start = ((s8[6815744]{0:T(1024)(128)(4,1)}), s8[4194304]{0:T(1024)(128)(4,1)S(1)}, s32[]{:S(2)}) async-start(s8[6815744]{0:T(1024)(128)(4,1)} %bitcast.136), calls=%async_computation.8 | async-start | bytes 8388608
  136.8 19.4 %copy-start.4 = (f32[16,8,100,100]{3,2,1,0:T(8,128)}, f32[16,8,100,100]{3,2,1,0:T(8,128)S(1)}, u32[]{:S(2)}) copy-start(f32[16,8,100,100]{3,2,1,0:T(8,128)S(1)} %fusion.35) | copy-start | bytes 15360004
  136.8 5.9 slice-start.1
  142.7 30.8 %copy-start.3 = (f32[16,8,100,100]{3,2,1,0:T(8,128)}, f32[16,8,100,100]{3,2,1,0:T(8,128)S(1)}, u32[]{:S(2)}) copy-start(f32[16,8,100,100]{3,2,1,0:T(8,128)S(1)} %fusion.32) | copy-start | bytes 15360004
  156.3 17.3 %copy-start.5 = (f32[16,8,100,100]{3,2,1,0:T(8,128)}, f32[16,8,100,100]{3,2,1,0:T(8,128)S(1)}, u32[]{:S(2)}) copy-start(f32[16,8,100,100]{3,2,1,0:T(8,128)S(1)} %fusion.38) | copy-start | bytes 15360004
  204.0 21.3 %slice-start.2 = ((s8[6815744]{0:T(1024)(128)(4,1)}), s8[2621440]{0:T(1024)(128)(4,1)S(1)}, s32[]{:S(2)}) async-start(s8[6815744]{0:T(1024)(128)(4,1)} %bitcast.138), calls=%async_computation.10 | async-start | bytes 5242880
  204.0 120.8 %all-to-all-start = ((f32[16,4,20000]{2,0,1:T(8,128)}), f32[16,4,20000]{2,0,1:T(8,128)}, u32[]{:S(2)}, u32[]{:S(2)}) async-start(f32[16,4,20000]{2,0,1:T(8,128)} %copy.65), calls=%async_computation | async-start | bytes 10289152 | tf_op jit(solution)/shard_map/all_to_all | solution.py:49
  210.8 14.5 %slice-start.3 = ((s8[6815744]{0:T(1024)(128)(4,1)}), s8[4194304]{0:T(1024)(128)(4,1)S(1)}, s32[]{:S(2)}) async-start(s8[6815744]{0:T(1024)(128)(4,1)} %bitcast.138), calls=%async_computation.11 | async-start | bytes 8388608
  256.3 73.5 %copy-start.7 = (f32[64,64]{1,0:T(8,128)S(1)}, f32[64,64]{1,0:T(8,128)}, u32[]{:S(2)}) copy-start(f32[64,64]{1,0:T(8,128)} %param.10) | copy-start | bytes 49156
  324.8 118.1 %all-to-all-start.1 = ((f32[16,4,20000]{2,0,1:T(8,128)}), f32[16,4,20000]{2,0,1:T(8,128)}, u32[]{:S(2)}, u32[]{:S(2)}) async-start(f32[16,4,20000]{2,0,1:T(8,128)} %copy.69), calls=%async_computation.1 | async-start | bytes 10289152 | tf_op jit(solution)/shard_map/all_to_all | solution.py:50
  329.8 113.1 %copy-start.8 = (f32[64,64]{1,0:T(8,128)S(1)}, f32[64,64]{1,0:T(8,128)}, u32[]{:S(2)}) copy-start(f32[64,64]{1,0:T(8,128)} %param.11) | copy-start | bytes 49156
  464.3 118.2 %all-to-all-start.2 = ((f32[64,1,20000]{2,1,0:T(1,128)}), f32[64,1,20000]{2,1,0:T(1,128)}, u32[]{:S(2)}, u32[]{:S(2)}) async-start(f32[64,1,20000]{2,1,0:T(1,128)} %copy.70), calls=%async_computation.2 | async-start | bytes 10289152 | tf_op jit(solution)/shard_map/all_to_all | solution.py:57
  582.4 118.5 %all-to-all-start.4 = ((f32[64,1,20000]{2,1,0:T(1,128)}), f32[64,1,20000]{2,1,0:T(1,128)}, u32[]{:S(2)}, u32[]{:S(2)}) async-start(f32[64,1,20000]{2,1,0:T(1,128)} %copy.74), calls=%async_computation.4 | async-start | bytes 10289152 | tf_op jit(solution)/shard_map/all_to_all | solution.py:60
  701.0 64.0 %all-to-all-start.3 = ((f32[8,8,20000]{2,0,1:T(8,128)}), f32[8,8,20000]{2,0,1:T(8,128)}, u32[]{:S(2)}, u32[]{:S(2)}) async-start(f32[8,8,20000]{2,0,1:T(8,128)} %copy.73), calls=%async_computation.3 | async-start | bytes 10289152 | tf_op jit(solution)/shard_map/all_to_all | solution.py:75
  764.9 63.9 %all-to-all-start.5 = ((f32[8,8,20000]{2,0,1:T(8,128)}), f32[8,8,20000]{2,0,1:T(8,128)}, u32[]{:S(2)}, u32[]{:S(2)}) async-start(f32[8,8,20000]{2,0,1:T(8,128)} %copy.77), calls=%async_computation.5 | async-start | bytes 10289152 | tf_op jit(solution)/shard_map/all_to_all | solution.py:76
  850.4 63.9 %all-to-all-start.6 = ((f32[64,1,20000]{2,1,0:T(1,128)}), f32[64,1,20000]{2,1,0:T(1,128)}, u32[]{:S(2)}, u32[]{:S(2)}) async-start(f32[64,1,20000]{2,1,0:T(1,128)} %copy.78), calls=%async_computation.6 | async-start | bytes 10289152 | tf_op jit(solution)/shard_map/all_to_all | solution.py:83
  914.3 64.0 %all-to-all-start.7 = ((f32[64,1,20000]{2,1,0:T(1,128)}), f32[64,1,20000]{2,1,0:T(1,128)}, u32[]{:S(2)}, u32[]{:S(2)}) async-start(f32[64,1,20000]{2,1,0:T(1,128)} %copy.81), calls=%async_computation.7 | async-start | bytes 10289152 | tf_op jit(solution)/shard_map/all_to_all | solution.py:89
  1029.4 27.2 %copy-start.1 = (f32[100,100]{1,0:T(8,128)S(1)}, f32[100,100]{1,0:T(8,128)}, u32[]{:S(2)}) copy-start(f32[100,100]{1,0:T(8,128)} %param.8) | copy-start | bytes 120004
where the time goes:
time: 1070 us; the launch traced here: 1060 us
  waiting for transfers between devices  498 us (47%)
  local copies, waits for them, and re-layouts  274 us (26%)
  matrix products  161 us (15%)
  other arithmetic  82.4 us (8%)
  starting transfers between devices  41.1 us (4%)
    all_to_all x1, waiting for transfers between devices, ket_side(): lax.all_to_all(shaped[1], 'row', split_axis=1, concat_axis=0, tiled=True)  103 us
    all_to_all x1, waiting for transfers between devices, ket_side(): lax.all_to_all(mixed[0], 'row', split_axis=0, concat_axis=1, tiled=True)  86.9 us
    unnamed x4, other arithmetic  82.4 us
    all_to_all x1, waiting for transfers between devices, ket_side(): lax.all_to_all(mixed[1], 'row', split_axis=0, concat_axis=1, tiled=True)  78.3 us
    all_to_all x1, waiting for transfers between devices, ket_side(): lax.all_to_all(shaped[0], 'row', split_axis=1, concat_axis=0, tiled=True)  68.5 us
    all_to_all x1, waiting for transfers between devices, bra_side(): lax.all_to_all(mixed[1], 'col', split_axis=0, concat_axis=1, tiled=True)  53.6 us
    all_to_all x1, waiting for transfers between devices, bra_side(): lax.all_to_all(moved_imag, 'col', split_axis=1, concat_axis=0, tiled=True)  49.6 us
    reshape x4, local copies, waits for them, and re-layouts, local(): state = (rho_real.reshape(shape_four), rho_imag.reshape(shape_four))  44.6 us
  transfers between devices with their start and end apart: 8, of which 8 were waited for; matrix products, arithmetic and copies ran while one was open for 18% of the time, Pallas kernels for 0%

commit v1 on v0

--- a/solution.py
+++ b/solution.py
@@ -5,6 +5,13 @@
 
 MECH = 64
 highest = lax.Precision.HIGHEST
+
+
+def exchange_blocks(x, axis, split, join):
+    peers = lax.axis_size(axis)
+    blocks = jnp.stack(jnp.split(x, peers, axis=split), axis=0)
+    blocks = lax.all_to_all(blocks, axis, split_axis=0, concat_axis=0)
+    return jnp.concatenate(blocks, axis=join)
 
 
 def cavity_sides(parts, cav_real, cav_imag):
@@ -86,9 +93,7 @@
         (1, 2, 0, 3),
     )
     back_imag = jnp.transpose(
-        lax.all_to_all(mixed[1], "col", split_axis=0, concat_axis=1, tiled=True).reshape(
-            local_cols, local_rows, cav_count, width
-        ),
+        exchange_blocks(mixed[1], "col", 0, 1).reshape(local_cols, local_rows, cav_count, width),
         (1, 2, 0, 3),
     )
     return (back_real, back_imag)

time: 1070 us -> 1030 us (0.963)
  waiting for transfers between devices: 498 us -> 467 us
    all_to_all x1, waiting for transfers between devices: 53.6 us -> 17 us  [exchange_blocks(): blocks = lax.all_to_all(blocks, axis, split_axis=0, concat_axis=0)]
  transfers between devices with their start and end apart: 8 -> 8, of which waited for: 8 -> 8; matrix products, arithmetic and copies ran while one was open for 18% -> 22% of each run, Pallas kernels for 0% -> 0%
where the time goes in v1:
time: 1030 us; the launch traced here: 1020 us
  waiting for transfers between devices  467 us (45%)
  local copies, waits for them, and re-layouts  271 us (26%)
  matrix products  158 us (15%)
  other arithmetic  82.4 us (8%)
  starting transfers between devices  41.1 us (4%)
    all_to_all x1, waiting for transfers between devices, ket_side(): lax.all_to_all(shaped[1], 'row', split_axis=1, concat_axis=0, tiled=True)  103 us
    all_to_all x1, waiting for transfers between devices, ket_side(): lax.all_to_all(mixed[0], 'row', split_axis=0, concat_axis=1, tiled=True)  86.9 us
    unnamed x4, other arithmetic  82.4 us
    all_to_all x1, waiting for transfers between devices, ket_side(): lax.all_to_all(mixed[1], 'row', split_axis=0, concat_axis=1, tiled=True)  78.3 us
    all_to_all x1, waiting for transfers between devices, ket_side(): lax.all_to_all(shaped[0], 'row', split_axis=1, concat_axis=0, tiled=True)  68.5 us
    all_to_all x1, waiting for transfers between devices, bra_side(): lax.all_to_all(moved_imag, 'col', split_axis=1, concat_axis=0, tiled=True)  49.6 us
    reshape x4, local copies, waits for them, and re-layouts, local(): state = (rho_real.reshape(shape_four), rho_imag.reshape(shape_four))  44.6 us
    all_to_all x1, waiting for transfers between devices, bra_side(): lax.all_to_all(mixed[0], 'col', split_axis=0, concat_axis=1, tiled=True)  38.8 us
  transfers between devices with their start and end apart: 8, of which 8 were waited for; matrix products, arithmetic and copies ran while one was open for 22% of the time, Pallas kernels for 0%

profile of v1, /device:TPU:0, one launch (start us, length us, event | category | flops | bytes accessed | tf_op | source)
XLA Modules:
  0.0 1020.5 jit_solution(1211714638985155818)
XLA Ops:
  1.2 41.2 %reduce.7 = f32[1280000]{0:T(1024)} reduce(f32[1,1,1280000]{2,1,0:T(1,128)} %param.6, f32[]{:T(128)} %broadcast.6), dimensions={0,1}, to_apply=%param.6.reduce_sub_computation.3 | reduce | bytes 10240004 | tf_op args[0]
  42.4 14.0 %reshape.95 = f32[16,100,8,100]{3,2,1,0:T(8,128)} reshape(f32[1280000]{0:T(1024)} %reduce.7) | data formatting | bytes 10240000 | tf_op jit(solution)/shard_map/reshape | solution.py:108
  56.4 8.3 copy.58
  64.6 41.2 %reduce.6 = f32[1280000]{0:T(1024)} reduce(f32[1,1,1280000]{2,1,0:T(1,128)} %param.7, f32[]{:T(128)} %broadcast.6), dimensions={0,1}, to_apply=%param.7.reduce_sub_computation.3 | reduce | bytes 10240004 | tf_op args[1]
  105.9 14.1 %reshape.96 = f32[16,100,8,100]{3,2,1,0:T(8,128)} reshape(f32[1280000]{0:T(1024)} %reduce.6) | data formatting | bytes 10240000 | tf_op jit(solution)/shard_map/reshape | solution.py:108
  120.0 8.3 copy.59
  128.3 8.5 fusion.43
  136.8 5.8 fusion.40
  142.7 7.7 fusion.38
  150.4 5.8 fusion.46
  156.3 17.2 %fusion.6 = f32[16,100,8,100]{3,1,2,0:T(8,128)} fusion(f32[16,8,100,100]{3,2,1,0:T(8,128)S(1)} %fusion.43, f32[16,8,100,100]{3,2,1,0:T(8,128)} %fusion.38, f32[100,100]{1,0:T(8,128)S(1)} %copy-done.6), kind=kOutput, calls=%fused_computation.10 | convolution fusion | flops 1537280000 | bytes 15400000 | tf_op jit(solution)/shard_map/mcne,fe->mcnf/dot_general | solution.py:25
  173.5 13.6 %fusion.22 = f32[16,100,8,100]{3,1,2,0:T(8,128)S(1)} fusion(f32[16,100,8,100]{3,1,2,0:T(8,128)} %fusion.6, f32[16,8,100,100]{3,2,1,0:T(8,128)S(1)} %fusion.46, f32[16,8,100,100]{3,2,1,0:T(8,128)S(1)} %fusion.40, f32[100,100]{1,0:T(8,128)S(1)} %copy-done), kind=kOutput, calls=%fused_computation.29 | convolution fusion | flops 1538560000 | bytes 20520000 | tf_op jit(solution)/shard_map/mcne,fe->mcnf/dot_general | solution.py:25
  190.9 7.9 reshape.97
  198.9 5.1 copy.65
  204.0 6.8 all-to-all-start
  210.8 14.5 %fusion.4 = f32[16,100,8,100]{3,1,2,0:T(8,128)S(1)} fusion(f32[16,8,100,100]{3,2,1,0:T(8,128)} %copy-done.4, f32[16,8,100,100]{3,2,1,0:T(8,128)} %fusion.38, f32[100,100]{1,0:T(8,128)S(1)} %copy-done), kind=kOutput, calls=%fused_computation.8 | convolution fusion | flops 1537280000 | bytes 15400000 | tf_op jit(solution)/shard_map/mcne,fe->mcnf/dot_general | solution.py:28
  225.4 14.1 %fusion.25 = f32[16,100,8,100]{3,1,2,0:T(8,128)S(1)} fusion(f32[16,100,8,100]{3,1,2,0:T(8,128)S(1)} %fusion.4, f32[16,8,100,100]{3,2,1,0:T(8,128)} %copy-done.5, f32[16,8,100,100]{3,2,1,0:T(8,128)S(1)} %bitcast.166, f32[100,100]{1,0:T(8,128)S(1)} %copy-done.6), kind=kOutput, calls=%fused_computation.30 | convolution fusion | flops 1538560000 | bytes 20520000 | tf_op jit(solution)/shard_map/mcne,fe->mcnf/dot_general | solution.py:28
  239.4 3.9 copy.68
  243.3 7.9 reshape.99
  251.2 5.1 copy.69
  256.3 68.5 %all-to-all-done = f32[16,4,20000]{2,0,1:T(8,128)} async-done(((f32[16,4,20000]{2,0,1:T(8,128)}), f32[16,4,20000]{2,0,1:T(8,128)}, u32[]{:S(2)}, u32[]{:S(2)}) %all-to-all-start) | async-done | bytes 5120032 | tf_op jit(solution)/shard_map/all_to_all | solution.py:56
  324.8 5.1 all-to-all-start.1
  329.9 9.6 fusion.48
  339.4 103.5 %all-to-all-done.1 = f32[16,4,20000]{2,0,1:T(8,128)} async-done(((f32[16,4,20000]{2,0,1:T(8,128)}), f32[16,4,20000]{2,0,1:T(8,128)}, u32[]{:S(2)}, u32[]{:S(2)}) %all-to-all-start.1) | async-done | bytes 5120032 | tf_op jit(solution)/shard_map/all_to_all | solution.py:57
  442.9 11.1 %fusion = f32[64,1,20000]{2,0,1:T(8,128)} fusion(f32[20000,64]{0,1:T(8,128)} %fusion.48, f32[64,20000]{1,0:T(8,128)} %bitcast.13, f32[64,64]{1,0:T(8,128)S(1)} %copy-done.8), kind=kOutput, calls=%fused_computation.4 | convolution fusion | flops 984320000 | bytes 15376384 | tf_op jit(solution)/shard_map/mn,nok->mok/dot_general | solution.py:37
  454.0 10.2 %copy.70 = f32[64,1,20000]{2,1,0:T(1,128)} copy(f32[64,1,20000]{2,0,1:T(8,128)} %fusion) | data formatting | bytes 10240000 | tf_op jit(solution)/shard_map/sub | solution.py:42
  464.3 5.0 all-to-all-start.2
  469.3 6.7 fusion.49
  476.0 9.6 fusion.1
  485.6 10.0 copy.74
  495.6 86.9 %all-to-all-done.2 = f32[64,1,20000]{2,1,0:T(1,128)} async-done(((f32[64,1,20000]{2,1,0:T(1,128)}), f32[64,1,20000]{2,1,0:T(1,128)}, u32[]{:S(2)}, u32[]{:S(2)}) %all-to-all-start.2) | async-done | bytes 5120032 | tf_op jit(solution)/shard_map/all_to_all | solution.py:64
  582.4 5.4 all-to-all-start.4
  587.9 6.7 copy.94
  594.6 8.6 reshape.101
  603.2 7.0 copy.72
  610.2 6.8 reshape.102
  617.0 5.7 copy.73
  622.7 78.3 %all-to-all-done.4 = f32[64,1,20000]{2,1,0:T(1,128)} async-done(((f32[64,1,20000]{2,1,0:T(1,128)}), f32[64,1,20000]{2,1,0:T(1,128)}, u32[]{:S(2)}, u32[]{:S(2)}) %all-to-all-start.4) | async-done | bytes 5120032 | tf_op jit(solution)/shard_map/all_to_all | solution.py:67
  701.0 4.7 all-to-all-start.3
  705.6 6.7 copy.93
  712.4 8.6 reshape.104
  721.0 7.0 copy.76
  728.0 6.9 reshape.105
  734.9 5.7 copy.77
  740.6 24.3 %all-to-all-done.3 = f32[8,8,20000]{2,0,1:T(8,128)} async-done(((f32[8,8,20000]{2,0,1:T(8,128)}), f32[8,8,20000]{2,0,1:T(8,128)}, u32[]{:S(2)}, u32[]{:S(2)}) %all-to-all-start.3) | async-done | bytes 5120032 | tf_op jit(solution)/shard_map/all_to_all | solution.py:82
  764.9 4.8 all-to-all-start.5
  769.8 9.5 fusion.13
  779.3 49.6 %all-to-all-done.5 = f32[8,8,20000]{2,0,1:T(8,128)} async-done(((f32[8,8,20000]{2,0,1:T(8,128)}), f32[8,8,20000]{2,0,1:T(8,128)}, u32[]{:S(2)}, u32[]{:S(2)}) %all-to-all-start.5) | async-done | bytes 5120032 | tf_op jit(solution)/shard_map/all_to_all | solution.py:83
  828.9 11.1 %fusion.2 = f32[64,1,20000]{2,0,1:T(8,128)} fusion(f32[20000,64]{0,1:T(8,128)} %fusion.13, f32[64,64]{1,0:T(8,128)S(1)} %copy-done.8, f32[8,8,20000]{2,0,1:T(8,128)} %all-to-all-done.5), kind=kOutput, calls=%fused_computation.6 | convolution fusion | flops 984320000 | bytes 15376384 | tf_op jit(solution)/shard_map/mn,nok->mok/dot_general | solution.py:37
  839.9 10.3 %copy.78 = f32[64,1,20000]{2,1,0:T(1,128)} copy(f32[64,1,20000]{2,0,1:T(8,128)} %fusion.2) | data formatting | bytes 10240000 | tf_op jit(solution)/shard_map/add | solution.py:41
  850.2 4.7 all-to-all-start.6
  854.9 6.7 fusion.15
  861.5 6.7 fusion.3
  875.4 38.8 %all-to-all-done.6 = f32[64,1,20000]{2,1,0:T(1,128)} async-done(((f32[64,1,20000]{2,1,0:T(1,128)}), f32[64,1,20000]{2,1,0:T(1,128)}, u32[]{:S(2)}, u32[]{:S(2)}) %all-to-all-start.6) | async-done | bytes 5120032 | tf_op jit(solution)/shard_map/all_to_all | solution.py:90
  914.1 4.7 all-to-all-start.7
  918.8 5.7 copy.92
  924.6 9.4 reshape.107
  934.0 9.5 copy.80
  943.5 17.6 %reshape.108 = f32[1,1,1280000]{2,1,0:T(1,128)} reshape(f32[16,100,8,100]{3,2,1,0:T(8,128)} %copy.80) | data formatting | bytes 10240000 | tf_op jit(solution)/shard_map/reshape | solution.py:111
  961.1 17.0 %all-to-all-done.7 = f32[8,8,1,20000]{3,1,2,0:T(8,128)} async-done(((f32[8,8,1,20000]{3,1,2,0:T(8,128)}), f32[8,8,1,20000]{3,1,2,0:T(8,128)}, u32[]{:S(2)}, u32[]{:S(2)}) %all-to-all-start.7) | async-done | bytes 5120032 | tf_op jit(solution)/shard_map/all_to_all | solution.py:13
  978.1 5.7 copy.81
  983.8 9.2 reshape_reshape.3
  993.1 9.5 copy.82
  1002.6 17.7 %reshape.110 = f32[1,1,1280000]{2,1,0:T(1,128)} reshape(f32[16,100,8,100]{3,2,1,0:T(8,128)} %copy.82) | data formatting | bytes 10240000 | tf_op jit(solution)/shard_map/reshape | solution.py:111
  (38 shorter events, 11.5 us)
Async XLA Ops:
  0.6 127.6 %copy-start = (f32[100,100]{1,0:T(8,128)S(1)}, f32[100,100]{1,0:T(8,128)}, u32[]{:S(2)}) copy-start(f32[100,100]{1,0:T(8,128)} %param.8) | copy-start | bytes 120004
  128.3 8.5 copy-start.2
  128.3 8.5 copy-start.6
  128.3 14.4 %slice-start = ((s8[6815744]{0:T(1024)(128)(4,1)}), s8[4194304]{0:T(1024)(128)(4,1)S(1)}, s32[]{:S(2)}) async-start(s8[6815744]{0:T(1024)(128)(4,1)} %bitcast.163), calls=%async_computation.8 | async-start | bytes 8388608
  136.8 19.4 %copy-start.4 = (f32[16,8,100,100]{3,2,1,0:T(8,128)}, f32[16,8,100,100]{3,2,1,0:T(8,128)S(1)}, u32[]{:S(2)}) copy-start(f32[16,8,100,100]{3,2,1,0:T(8,128)S(1)} %fusion.43) | copy-start | bytes 15360004
  136.8 5.9 slice-start.1
  142.7 30.8 %copy-start.3 = (f32[16,8,100,100]{3,2,1,0:T(8,128)}, f32[16,8,100,100]{3,2,1,0:T(8,128)S(1)}, u32[]{:S(2)}) copy-start(f32[16,8,100,100]{3,2,1,0:T(8,128)S(1)} %fusion.40) | copy-start | bytes 15360004
  156.3 17.3 %copy-start.5 = (f32[16,8,100,100]{3,2,1,0:T(8,128)}, f32[16,8,100,100]{3,2,1,0:T(8,128)S(1)}, u32[]{:S(2)}) copy-start(f32[16,8,100,100]{3,2,1,0:T(8,128)S(1)} %fusion.46) | copy-start | bytes 15360004
  204.0 21.3 %slice-start.2 = ((s8[6815744]{0:T(1024)(128)(4,1)}), s8[2621440]{0:T(1024)(128)(4,1)S(1)}, s32[]{:S(2)}) async-start(s8[6815744]{0:T(1024)(128)(4,1)} %bitcast.165), calls=%async_computation.10 | async-start | bytes 5242880
  204.0 120.8 %all-to-all-start = ((f32[16,4,20000]{2,0,1:T(8,128)}), f32[16,4,20000]{2,0,1:T(8,128)}, u32[]{:S(2)}, u32[]{:S(2)}) async-start(f32[16,4,20000]{2,0,1:T(8,128)} %copy.65), calls=%async_computation | async-start | bytes 10289152 | tf_op jit(solution)/shard_map/all_to_all | solution.py:56
  210.8 14.5 %slice-start.3 = ((s8[6815744]{0:T(1024)(128)(4,1)}), s8[4194304]{0:T(1024)(128)(4,1)S(1)}, s32[]{:S(2)}) async-start(s8[6815744]{0:T(1024)(128)(4,1)} %bitcast.165), calls=%async_computation.11 | async-start | bytes 8388608
  256.3 73.5 %copy-start.7 = (f32[64,64]{1,0:T(8,128)S(1)}, f32[64,64]{1,0:T(8,128)}, u32[]{:S(2)}) copy-start(f32[64,64]{1,0:T(8,128)} %param.10) | copy-start | bytes 49156
  324.8 118.1 %all-to-all-start.1 = ((f32[16,4,20000]{2,0,1:T(8,128)}), f32[16,4,20000]{2,0,1:T(8,128)}, u32[]{:S(2)}, u32[]{:S(2)}) async-start(f32[16,4,20000]{2,0,1:T(8,128)} %copy.69), calls=%async_computation.1 | async-start | bytes 10289152 | tf_op jit(solution)/shard_map/all_to_all | solution.py:57
  329.8 113.1 %copy-start.8 = (f32[64,64]{1,0:T(8,128)S(1)}, f32[64,64]{1,0:T(8,128)}, u32[]{:S(2)}) copy-start(f32[64,64]{1,0:T(8,128)} %param.11) | copy-start | bytes 49156
  464.3 118.2 %all-to-all-start.2 = ((f32[64,1,20000]{2,1,0:T(1,128)}), f32[64,1,20000]{2,1,0:T(1,128)}, u32[]{:S(2)}, u32[]{:S(2)}) async-start(f32[64,1,20000]{2,1,0:T(1,128)} %copy.70), calls=%async_computation.2 | async-start | bytes 10289152 | tf_op jit(solution)/shard_map/all_to_all | solution.py:64
  582.4 118.5 %all-to-all-start.4 = ((f32[64,1,20000]{2,1,0:T(1,128)}), f32[64,1,20000]{2,1,0:T(1,128)}, u32[]{:S(2)}, u32[]{:S(2)}) async-start(f32[64,1,20000]{2,1,0:T(1,128)} %copy.74), calls=%async_computation.4 | async-start | bytes 10289152 | tf_op jit(solution)/shard_map/all_to_all | solution.py:67
  701.0 64.0 %all-to-all-start.3 = ((f32[8,8,20000]{2,0,1:T(8,128)}), f32[8,8,20000]{2,0,1:T(8,128)}, u32[]{:S(2)}, u32[]{:S(2)}) async-start(f32[8,8,20000]{2,0,1:T(8,128)} %copy.73), calls=%async_computation.3 | async-start | bytes 10289152 | tf_op jit(solution)/shard_map/all_to_all | solution.py:82
  764.9 64.0 %all-to-all-start.5 = ((f32[8,8,20000]{2,0,1:T(8,128)}), f32[8,8,20000]{2,0,1:T(8,128)}, u32[]{:S(2)}, u32[]{:S(2)}) async-start(f32[8,8,20000]{2,0,1:T(8,128)} %copy.77), calls=%async_computation.5 | async-start | bytes 10289152 | tf_op jit(solution)/shard_map/all_to_all | solution.py:83
  850.2 63.9 %all-to-all-start.6 = ((f32[64,1,20000]{2,1,0:T(1,128)}), f32[64,1,20000]{2,1,0:T(1,128)}, u32[]{:S(2)}, u32[]{:S(2)}) async-start(f32[64,1,20000]{2,1,0:T(1,128)} %copy.78), calls=%async_computation.6 | async-start | bytes 10289152 | tf_op jit(solution)/shard_map/all_to_all | solution.py:90
  914.1 64.0 %all-to-all-start.7 = ((f32[8,8,1,20000]{3,1,2,0:T(8,128)}), f32[8,8,1,20000]{3,1,2,0:T(8,128)}, u32[]{:S(2)}, u32[]{:S(2)}) async-start(f32[8,8,1,20000]{3,1,2,0:T(8,128)} %fusion.28), calls=%async_computation.7 | async-start | bytes 10289152 | tf_op jit(solution)/shard_map/all_to_all | solution.py:13
  993.1 27.2 %copy-start.1 = (f32[100,100]{1,0:T(8,128)S(1)}, f32[100,100]{1,0:T(8,128)}, u32[]{:S(2)}) copy-start(f32[100,100]{1,0:T(8,128)} %param.8) | copy-start | bytes 120004
